TPU v7x, 32 devices: a whole 2x2x4 slice. The times are simulated.
32 devices in a mesh: groups: 2 (over y), gx: 4 (over z), gy: 2 (over x), gz: 2 (over core).
Axes of the slice: x: 2, y: 2, z: 4, core: 2. Of those that a mesh axis runs over, the one named last changes fastest.
Arguments:
- earlier_warmth_field: float32 [16, 512, 512], P(('groups', 'gz'), 'gy', 'gx'), parts along dimension 0, may hold values from -6 to 6
- caloric_storage: float32 [16, 512, 512], P(('groups', 'gz'), 'gy', 'gx'), parts along dimension 0, may hold values from 0.5 to 4
- thermal_diffusivity_coefficient: float32 [16, 512, 512], P(('groups', 'gz'), 'gy', 'gx'), parts along dimension 0, may hold values from 0.3 to 3
- dissipation_catalog: float32 [16, 64, 128], P('groups'), parts along dimension 0, may hold values from 0.1 to 3
- dissipation_selector: int32 [16, 8, 4], P(('groups', 'gz'), 'gy', 'gx'), parts along dimension 0, may hold values from 0 to 7
- refine_depth: int32 [16, 8, 4], P(('groups', 'gz'), 'gy', 'gx'), parts along dimension 0, may hold values from 1 to 4, as said below
- border_band_width: int32 [16, 4], P(('groups', 'gy'), 'gx'), parts along dimension 0, may hold values from 1 to 16
- microflow_flag: int32 [16], P(('groups', 'gz')), parts along dimension 0, may hold values 0 or 1
Outputs:
- warmth_solution: float32 [16, 512, 512], P(('groups', 'gz'), 'gy', 'gx'), parts along dimension 0
- leftover_misfit: float32 [16, 512, 512], P(('groups', 'gz'), 'gy', 'gx'), parts along dimension 0
There are 2 independent parts, one for each index of `groups`. A program takes and returns all parts, laid end to end along the dimension named above; each array names one. Nothing has to cross between parts.
Inputs may be any that keep to these rules, and one draw needn't show every extreme that they name: `refine_depth`: each tile's level is 1, 2 or 4.
All inputs are finite; a program needn't handle non-finite values. No bound on the sum of `microflow_flag` on one device may be relied on, other than what follows from the above.
Results may differ from a plain program's by a relative error of at most 0.00022.
Values sent between devices are 32-bit elements; how exact they have to be, the bound alone decides.
No kernel may reach another device: no remote copies, remote signals or barrier semaphores. Data moves between devices by JAX's collectives and lax.ppermute only.
A program may use at most 64 MiB of HBM per device.

v0:
```python
import jax
import jax.numpy as jnp
from jax import lax
from jax.sharding import PartitionSpec as P

TY = 64
ITERS = 2
interval_increment = 0.5
vertical_ratio = 2.0
coolant_film = 1.5
band_sink = 1.0
damping = 0.8


def with_halo(shard, sides, width):
    for axis, dim in sides:
        count, length = (lax.axis_size(axis), shard.shape[dim])
        up = [(i, (i + 1) % count) for i in range(count - 1)]
        down = [(j, i) for i, j in up]
        last = lax.slice_in_dim(shard, length - width, length, axis=dim)
        first = lax.slice_in_dim(shard, 0, width, axis=dim)
        before = lax.ppermute(last, axis, up)
        after = lax.ppermute(first, axis, down)
        shard = jnp.concatenate([before, shard, after], axis=dim)
    return shard


def harmonic(first, second):
    return 2.0 * first * second / (first + second)


def neighbours(padded):
    return (
        padded[:-2, 1:-1, 1:-1],
        padded[2:, 1:-1, 1:-1],
        padded[1:-1, :-2, 1:-1],
        padded[1:-1, 2:, 1:-1],
        padded[1:-1, 1:-1, :-2],
        padded[1:-1, 1:-1, 2:],
    )


def body(
    earlier_warmth_field,
    caloric_storage,
    thermal_diffusivity_coefficient,
    dissipation_catalog,
    dissipation_selector,
    refine_depth,
    border_band_width,
    microflow_flag,
):
    stacked_layers, vertical_count, horizontal_count = earlier_warmth_field.shape
    kappa_rim = with_halo(thermal_diffusivity_coefficient, (("gx", 2), ("gy", 1), ("gz", 0)), 1)
    faces = [harmonic(thermal_diffusivity_coefficient, other) for other in neighbours(kappa_rim)]
    faces[0] = vertical_ratio * faces[0]
    faces[1] = vertical_ratio * faces[1]
    edge_cells = jnp.repeat(border_band_width, TY, axis=0)
    row_tile = (jnp.arange(vertical_count, dtype=jnp.int32) % TY)[:, None]
    band = ((row_tile < edge_cells) | (row_tile >= TY - edge_cells)).astype(jnp.float32)
    sink = coolant_film * microflow_flag.astype(jnp.float32)[:, None, None] + band_sink * band[None]
    diagonal = caloric_storage / interval_increment + sink
    for face in faces:
        diagonal = diagonal + face
    column_patch = jnp.arange(horizontal_count, dtype=jnp.int32)
    tile_faces = (
        faces[2] * (row_tile != 0).astype(jnp.float32),
        faces[3] * (row_tile != TY - 1).astype(jnp.float32),
        faces[4] * (column_patch != 0).astype(jnp.float32),
        faces[5] * (column_patch != horizontal_count - 1).astype(jnp.float32),
    )
    level_cells = jnp.repeat(refine_depth, TY, axis=1)
    map_count = dissipation_catalog.shape[0]
    onehot = (dissipation_selector[:, :, 0, None] == jnp.arange(map_count, dtype=jnp.int32)).astype(
        jnp.float32
    )
    dissipation_density = jnp.einsum(
        "zjp,pyx->zjyx", onehot, dissipation_catalog, precision=lax.Precision.HIGHEST
    ).reshape(stacked_layers, vertical_count, horizontal_count)
    linear_source_term = (
        caloric_storage / interval_increment * earlier_warmth_field + dissipation_density
    )

    def linear_map_action(field):
        padded = with_halo(field, (("gx", 2), ("gy", 1), ("gz", 0)), 1)
        total = diagonal * field
        for face, other in zip(faces, neighbours(padded)):
            total = total - face * other
        return total

    def smooth(vector):
        state = damping * vector / diagonal
        for sweep in range(1, 4):
            padded = jnp.pad(state, ((0, 0), (1, 1), (1, 1)))
            inner = tile_faces[0] * padded[:, :-2, 1:-1] + tile_faces[1] * padded[:, 2:, 1:-1]
            inner = (
                inner + tile_faces[2] * padded[:, 1:-1, :-2] + tile_faces[3] * padded[:, 1:-1, 2:]
            )
            fresh = (1.0 - damping) * state + damping * (vector + inner) / diagonal
            state = jnp.where(level_cells > sweep, fresh, state)
        return state

    warmth_solution = earlier_warmth_field
    leftover_misfit = linear_source_term - linear_map_action(warmth_solution)
    smoothed = smooth(leftover_misfit)
    applied = linear_map_action(smoothed)
    for turn in range(ITERS):
        gamma_now, delta_now = lax.psum(
            (jnp.sum(leftover_misfit * smoothed), jnp.sum(applied * smoothed)), ("gx", "gy", "gz")
        )
        pre = smooth(applied)
        twice = linear_map_action(pre)
        if turn == 0:
            present_stride_amount = gamma_now / delta_now
            image_dir, smooth_dir, operator_times_direction, conjugate_update_heading = (
                twice,
                pre,
                applied,
                smoothed,
            )
        else:
            current_mixing_factor = gamma_now / gamma_prev
            present_stride_amount = gamma_now / (
                delta_now - current_mixing_factor * gamma_now / alpha_prev
            )
            image_dir = twice + current_mixing_factor * image_dir
            smooth_dir = pre + current_mixing_factor * smooth_dir
            operator_times_direction = applied + current_mixing_factor * operator_times_direction
            conjugate_update_heading = smoothed + current_mixing_factor * conjugate_update_heading
        warmth_solution = warmth_solution + present_stride_amount * conjugate_update_heading
        leftover_misfit = leftover_misfit - present_stride_amount * operator_times_direction
        if turn + 1 < ITERS:
            smoothed = smoothed - present_stride_amount * smooth_dir
            applied = linear_map_action(smoothed)
        gamma_prev, alpha_prev = (gamma_now, present_stride_amount)
    return (warmth_solution, leftover_misfit)


def solution(mesh):
    return jax.shard_map(
        body,
        mesh=mesh,
        in_specs=(
            P(("groups", "gz"), "gy", "gx"),
            P(("groups", "gz"), "gy", "gx"),
            P(("groups", "gz"), "gy", "gx"),
            P("groups", None, None),
            P(("groups", "gz"), "gy", "gx"),
            P(("groups", "gz"), "gy", "gx"),
            P(("groups", "gy"), "gx"),
            P(("groups", "gz")),
        ),
        out_specs=(P(("groups", "gz"), "gy", "gx"), P(("groups", "gz"), "gy", "gx")),
        check_vma=False,
    )
```

profile of v0, /device:TPU:0, one launch (start us, length us, event | category | flops | bytes accessed | tf_op | source)
XLA Modules:
  0.0 202.6 jit_solution(9930890958993695138)
XLA Ops:
  0.6 2.4 %fusion.120 = (f32[4,256,1]{2,1,0:T(8,128)}, f32[4,256,1]{2,1,0:T(8,128)}) fusion(f32[4,256,128]{2,1,0:T(8,128)} %param.10), kind=kLoop, calls=%fused_computation.277 | loop fusion | bytes 16384 | tf_op jit(solution)/shard_map/slice | solution.py:20
  3.0 5.0 %collective-permute-start = (f32[4,256,1]{2,1,0:T(8,128)}, f32[4,256,1]{2,1,0:T(8,128)S(1)}, u32[]{:S(2)}, u32[]{:S(2)}) collective-permute-start(f32[4,256,1]{2,1,0:T(8,128)} %get-tuple-element.41), channel_id=1, source_target_pairs={{0,4},{4,8},{8,12},{1,5},{5,9},{9,13},{2,6},{6,10},{10,14},{3,7},{... | collective-permute-start | bytes 12296 | tf_op jit(solution)/shard_map/ppermute | solution.py:22
  8.1 1.4 collective-permute-start.1
  10.6 4.7 %collective-permute-start.6 = (f32[4,256,1]{2,1,0:T(8,128)}, f32[4,256,1]{2,1,0:T(8,128)S(1)}, u32[]{:S(2)}, u32[]{:S(2)}) collective-permute-start(f32[4,256,1]{2,1,0:T(8,128)} %get-tuple-element.43), channel_id=1, source_target_pairs={{0,4},{4,8},{8,12},{1,5},{5,9},{9,13},{2,6},{6,10},{10,14},{3,7},{... | collective-permute-start | bytes 12296 | tf_op jit(solution)/shard_map/ppermute | solution.py:22
  17.5 3.1 %collective-permute-done = f32[4,256,1]{2,1,0:T(8,128)S(1)} collective-permute-done((f32[4,256,1]{2,1,0:T(8,128)}, f32[4,256,1]{2,1,0:T(8,128)S(1)}, u32[]{:S(2)}, u32[]{:S(2)}) %collective-permute-start) | collective-permute-done | bytes 4128 | tf_op jit(solution)/shard_map/ppermute | solution.py:22
  20.6 4.5 %collective-permute-done.1 = f32[4,256,1]{2,1,0:T(8,128)S(1)} collective-permute-done((f32[4,256,1]{2,1,0:T(8,128)}, f32[4,256,1]{2,1,0:T(8,128)S(1)}, u32[]{:S(2)}, u32[]{:S(2)}) %collective-permute-start.1) | collective-permute-done | bytes 4128 | tf_op jit(solution)/shard_map/ppermute | solution.py:23
  25.2 3.4 %collective-permute-start.2 = (f32[4,1,130]{2,1,0:T(1,128)S(1)}, f32[4,1,130]{2,1,0:T(1,128)S(1)}, u32[]{:S(2)}, u32[]{:S(2)}) collective-permute-start(f32[4,1,130]{2,1,0:T(1,128)S(1)} %get-tuple-element.33), channel_id=1, source_target_pairs={{0,2},{1,3},{4,6},{5,7},{8,10},{9,11},{12,14},{13,15},{16,18},{17,... | collective-permute-start | bytes 6248 | tf_op jit(solution)/shard_map/ppermute | solution.py:22
  30.7 4.2 %collective-permute-done.7 = f32[4,256,1]{2,1,0:T(8,128)S(1)} collective-permute-done((f32[4,256,1]{2,1,0:T(8,128)}, f32[4,256,1]{2,1,0:T(8,128)S(1)}, u32[]{:S(2)}, u32[]{:S(2)}) %collective-permute-start.7) | collective-permute-done | bytes 4128 | tf_op jit(solution)/shard_map/ppermute | solution.py:23
  35.0 3.4 %collective-permute-start.8 = (f32[4,1,130]{2,1,0:T(1,128)S(1)}, f32[4,1,130]{2,1,0:T(1,128)S(1)}, u32[]{:S(2)}, u32[]{:S(2)}) collective-permute-start(f32[4,1,130]{2,1,0:T(1,128)S(1)} %get-tuple-element.35), channel_id=1, source_target_pairs={{0,2},{1,3},{4,6},{5,7},{8,10},{9,11},{12,14},{13,15},{16,18},{17,... | collective-permute-start | bytes 6248 | tf_op jit(solution)/shard_map/ppermute | solution.py:22
  44.2 2.6 %collective-permute-start.10 = (f32[1,258,130]{2,1,0:T(8,128)S(1)}, f32[1,258,130]{2,1,0:T(8,128)S(1)}, u32[]{:S(2)}, u32[]{:S(2)}) collective-permute-start(f32[1,258,130]{2,1,0:T(8,128)S(1)} %get-tuple-element.27), channel_id=1, source_target_pairs={{0,1},{2,3},{4,5},{6,7},{8,9},{10,11},{12,13},{14,15},{16,17},{18,... | collective-permute-start | bytes 402488 | tf_op jit(solution)/shard_map/ppermute | solution.py:22
  51.0 7.1 %multiply_divide_fusion.1 = (f32[4,256,128]{2,1,0:T(8,128)S(1)}, f32[4,256,128]{2,1,0:T(8,128)S(1)}, f32[4,256,128]{2,1,0:T(8,128)S(1)}, f32[4,256,128]{2,1,0:T(...) fusion(f32[4,256,1]{2,1,0:T(8,128)} %copy-done.16, ...), kind=kLoop, calls=%fused_computation.215 | loop fusion | flops 10878976 | bytes 7381184 | tf_op jit(solution)/shard_map/div | solution.py:92
  60.0 3.5 %collective-permute-start.12 = (f32[4,256,1]{2,1,0:T(8,128)S(1)}, f32[4,256,1]{2,1,0:T(8,128)S(1)}, u32[]{:S(2)}, u32[]{:S(2)}) collective-permute-start(f32[4,256,1]{2,1,0:T(8,128)S(1)} %get-tuple-element.39), channel_id=1, source_target_pairs={{0,4},{4,8},{8,12},{1,5},{5,9},{9,13},{2,6},{6,10},{10,14},{3,7},{... | collective-permute-start | bytes 12296 | tf_op jit(solution)/shard_map/ppermute | solution.py:22
  64.8 10.1 %collective-permute-done.12 = f32[4,256,1]{2,1,0:T(8,128)S(1)} collective-permute-done((f32[4,256,1]{2,1,0:T(8,128)S(1)}, f32[4,256,1]{2,1,0:T(8,128)S(1)}, u32[]{:S(2)}, u32[]{:S(2)}) %collective-permute-start.12) | collective-permute-done | bytes 4128 | tf_op jit(solution)/shard_map/ppermute | solution.py:22
  74.9 4.7 %collective-permute-done.13 = f32[4,256,1]{2,1,0:T(8,128)S(1)} collective-permute-done((f32[4,256,1]{2,1,0:T(8,128)S(1)}, f32[4,256,1]{2,1,0:T(8,128)S(1)}, u32[]{:S(2)}, u32[]{:S(2)}) %collective-permute-start.13) | collective-permute-done | bytes 4128 | tf_op jit(solution)/shard_map/ppermute | solution.py:23
  79.7 4.5 %collective-permute-start.14 = (f32[4,1,130]{2,1,0:T(1,128)S(1)}, f32[4,1,130]{2,1,0:T(1,128)S(1)}, u32[]{:S(2)}, u32[]{:S(2)}) collective-permute-start(f32[4,1,130]{2,1,0:T(1,128)S(1)} %get-tuple-element.31), channel_id=1, source_target_pairs={{0,2},{1,3},{4,6},{5,7},{8,10},{9,11},{12,14},{13,15},{16,18},{17,... | collective-permute-start | bytes 6248 | tf_op jit(solution)/shard_map/ppermute | solution.py:22
  85.6 4.2 %collective-permute-done.15 = f32[4,1,130]{2,1,0:T(1,128)S(1)} collective-permute-done((f32[4,1,130]{2,1,0:T(1,128)S(1)}, f32[4,1,130]{2,1,0:T(1,128)S(1)}, u32[]{:S(2)}, u32[]{:S(2)}) %collective-permute-start.15) | collective-permute-done | bytes 2112 | tf_op jit(solution)/shard_map/ppermute | solution.py:23
  90.1 1.3 collective-permute-start.16
  92.7 2.1 %collective-permute-done.17 = f32[1,258,130]{2,1,0:T(8,128)S(1)} collective-permute-done((f32[1,258,130]{2,1,0:T(8,128)S(1)}, f32[1,258,130]{2,1,0:T(8,128)S(1)}, u32[]{:S(2)}, u32[]{:S(2)}) %collective-permute-start.17) | collective-permute-done | bytes 134192 | tf_op jit(solution)/shard_map/ppermute | solution.py:23
  94.8 1.7 multiply_reduce_fusion.2
  97.4 1.4 fusion.56
  98.7 30.3 %all-reduce.7 = (f32[]{:T(128)}, f32[]{:T(128)}) all-reduce(f32[]{:T(128)} %get-tuple-element.5, f32[]{:T(128)} %get-tuple-element.4), channel_id=1, replica_groups=mesh['groups'=2,'gx'=4,'gy'=2,'gz'=2] {'gx','gy','gz'}, use_global_device_ids=true, to_apply=%region_1.2 | all-reduce | flops 2 | bytes 16 | tf_op jit(solution)/shard_map/psum | solution.py:108
  130.3 2.9 %multiply_subtract_fusion.1 = f32[4,256,128]{2,1,0:T(8,128)S(1)} fusion(f32[4,256,128]{2,1,0:T(8,128)S(1)} %fusion.32, f32[4,256,128]{2,1,0:T(8,128)} %fusion.56, f32[4,256,128]{2,1,0:T(8,128)S(1)} %get-tuple-element.14, f32[4,256,128]{2,1,0:T(8,128)} %copy-done.3, f32[4,256,128]{2,1,0:T(8,128)S(1)} %get-tuple-element.20, ...), kind=kLoop, calls=%fused_computation.210 | loop fusion | flops 2490368 | bytes 4722692 | tf_op jit(solution)/shard_map/sub | solution.py:133
  133.4 1.3 collective-permute-start.18
  136.0 10.0 %collective-permute-done.18 = f32[4,256,1]{2,1,0:T(8,128)S(1)} collective-permute-done((f32[4,256,1]{2,1,0:T(8,128)S(1)}, f32[4,256,1]{2,1,0:T(8,128)S(1)}, u32[]{:S(2)}, u32[]{:S(2)}) %collective-permute-start.18) | collective-permute-done | bytes 4128 | tf_op jit(solution)/shard_map/ppermute | solution.py:22
  146.0 4.1 %collective-permute-done.19 = f32[4,256,1]{2,1,0:T(8,128)S(1)} collective-permute-done((f32[4,256,1]{2,1,0:T(8,128)S(1)}, f32[4,256,1]{2,1,0:T(8,128)S(1)}, u32[]{:S(2)}, u32[]{:S(2)}) %collective-permute-start.19) | collective-permute-done | bytes 4128 | tf_op jit(solution)/shard_map/ppermute | solution.py:23
  151.6 1.4 collective-permute-start.21
  153.0 4.2 %collective-permute-done.21 = f32[4,1,130]{2,1,0:T(1,128)S(1)} collective-permute-done((f32[4,1,130]{2,1,0:T(1,128)S(1)}, f32[4,1,130]{2,1,0:T(1,128)S(1)}, u32[]{:S(2)}, u32[]{:S(2)}) %collective-permute-start.21) | collective-permute-done | bytes 2112 | tf_op jit(solution)/shard_map/ppermute | solution.py:23
  157.5 1.3 collective-permute-start.22
  160.1 2.1 %collective-permute-done.23 = f32[1,258,130]{2,1,0:T(8,128)S(1)} collective-permute-done((f32[1,258,130]{2,1,0:T(8,128)S(1)}, f32[1,258,130]{2,1,0:T(8,128)S(1)}, u32[]{:S(2)}, u32[]{:S(2)}) %collective-permute-start.23) | collective-permute-done | bytes 134192 | tf_op jit(solution)/shard_map/ppermute | solution.py:23
  162.3 2.5 %multiply_reduce_fusion = (f32[]{:T(128)}, f32[]{:T(128)}, f32[4,256,128]{2,1,0:T(8,128)}) fusion(f32[4,256,128]{2,1,0:T(8,128)S(1)} %multiply_subtract_fusion.1, f32[4,256,128]{2,1,0:T(8,128)S(1)} %copy-done.1, f32[4,256,128]{2,1,0:T(8,128)S(1)} %copy-done.4, f32[]{:T(128)S(6)} %div.69, f32[4,256,128]{2,1,0:T(8,128)S(1)} %get-tuple-element.20, ...), kind=kLoop, calls=%fused_computation.208 | loop fusion | flops 4849662 | bytes 6047852 | tf_op jit(solution)/shard_map/reduce_sum | solution.py:109
  164.8 30.2 %all-reduce.6 = (f32[]{:T(128)}, f32[]{:T(128)}) all-reduce(f32[]{:T(128)} %get-tuple-element.3, f32[]{:T(128)} %get-tuple-element.2), channel_id=1, replica_groups=mesh['groups'=2,'gx'=4,'gy'=2,'gz'=2] {'gx','gy','gz'}, use_global_device_ids=true, to_apply=%region_5.6 | all-reduce | flops 2 | bytes 16 | tf_op jit(solution)/shard_map/psum | solution.py:108
  199.4 2.2 %multiply_add_fusion = f32[4,256,128]{2,1,0:T(8,128)} fusion(f32[4,256,128]{2,1,0:T(8,128)} %copy-done.6, f32[4,256,128]{2,1,0:T(8,128)S(1)} %fusion.32, f32[4,256,128]{2,1,0:T(8,128)} %param.8, f32[]{:T(128)S(6)} %div.74, f32[]{:T(128)S(6)} %div.76, f32[]{:T(128)S(6)} %div.69), kind=kLoop, calls=%fused_computation.207 | loop fusion | flops 786432 | bytes 2097164 | tf_op jit(solution)/shard_map/add | solution.py:130
  (110 shorter events, 27.7 us)
Async XLA Ops:
  3.0 17.6 %collective-permute-start = (f32[4,256,1]{2,1,0:T(8,128)}, f32[4,256,1]{2,1,0:T(8,128)S(1)}, u32[]{:S(2)}, u32[]{:S(2)}) collective-permute-start(f32[4,256,1]{2,1,0:T(8,128)} %get-tuple-element.41), channel_id=1, source_target_pairs={{0,4},{4,8},{8,12},{1,5},{5,9},{9,13},{2,6},{6,10},{10,14},{3,7},{... | collective-permute-start | bytes 12296 | tf_op jit(solution)/shard_map/ppermute | solution.py:22
  8.1 17.0 %collective-permute-start.1 = (f32[4,256,1]{2,1,0:T(8,128)}, f32[4,256,1]{2,1,0:T(8,128)S(1)}, u32[]{:S(2)}, u32[]{:S(2)}) collective-permute-start(f32[4,256,1]{2,1,0:T(8,128)} %get-tuple-element.42), channel_id=1, source_target_pairs={{4,0},{8,4},{12,8},{5,1},{9,5},{13,9},{6,2},{10,6},{14,10},{7,3},{... | collective-permute-start | bytes 12296 | tf_op jit(solution)/shard_map/ppermute | solution.py:23
  10.6 14.5 %copy-start.8 = (f32[4,256,128]{2,1,0:T(8,128)S(1)}, f32[4,256,128]{2,1,0:T(8,128)}, u32[]{:S(2)}) copy-start(f32[4,256,128]{2,1,0:T(8,128)} %param.10) | copy-start | bytes 1572868
  10.6 20.1 %collective-permute-start.6 = (f32[4,256,1]{2,1,0:T(8,128)}, f32[4,256,1]{2,1,0:T(8,128)S(1)}, u32[]{:S(2)}, u32[]{:S(2)}) collective-permute-start(f32[4,256,1]{2,1,0:T(8,128)} %get-tuple-element.43), channel_id=1, source_target_pairs={{0,4},{4,8},{8,12},{1,5},{5,9},{9,13},{2,6},{6,10},{10,14},{3,7},{... | collective-permute-start | bytes 12296 | tf_op jit(solution)/shard_map/ppermute | solution.py:22
  15.3 19.6 %collective-permute-start.7 = (f32[4,256,1]{2,1,0:T(8,128)}, f32[4,256,1]{2,1,0:T(8,128)S(1)}, u32[]{:S(2)}, u32[]{:S(2)}) collective-permute-start(f32[4,256,1]{2,1,0:T(8,128)} %get-tuple-element.44), channel_id=1, source_target_pairs={{4,0},{8,4},{12,8},{5,1},{9,5},{13,9},{6,2},{10,6},{14,10},{7,3},{... | collective-permute-start | bytes 12296 | tf_op jit(solution)/shard_map/ppermute | solution.py:23
  20.6 19.2 %copy-start.13 = (f32[4,256,1]{2,1,0:T(8,128)}, f32[4,256,1]{2,1,0:T(8,128)S(1)}, u32[]{:S(2)}) copy-start(f32[4,256,1]{2,1,0:T(8,128)S(1)} %collective-permute-done) | copy-start | bytes 12292
  25.1 14.7 %copy-start.14 = (f32[4,256,1]{2,1,0:T(8,128)}, f32[4,256,1]{2,1,0:T(8,128)S(1)}, u32[]{:S(2)}) copy-start(f32[4,256,1]{2,1,0:T(8,128)S(1)} %collective-permute-done.1) | copy-start | bytes 12292
  25.2 14.5 %collective-permute-start.2 = (f32[4,1,130]{2,1,0:T(1,128)S(1)}, f32[4,1,130]{2,1,0:T(1,128)S(1)}, u32[]{:S(2)}, u32[]{:S(2)}) collective-permute-start(f32[4,1,130]{2,1,0:T(1,128)S(1)} %get-tuple-element.33), channel_id=1, source_target_pairs={{0,2},{1,3},{4,6},{5,7},{8,10},{9,11},{12,14},{13,15},{16,18},{17,... | collective-permute-start | bytes 6248 | tf_op jit(solution)/shard_map/ppermute | solution.py:22
  28.6 11.1 %collective-permute-start.3 = (f32[4,1,130]{2,1,0:T(1,128)S(1)}, f32[4,1,130]{2,1,0:T(1,128)S(1)}, u32[]{:S(2)}, u32[]{:S(2)}) collective-permute-start(f32[4,1,130]{2,1,0:T(1,128)S(1)} %get-tuple-element.34), channel_id=1, source_target_pairs={{2,0},{3,1},{6,4},{7,5},{10,8},{11,9},{14,12},{15,13},{18,16},{19,... | collective-permute-start | bytes 6248 | tf_op jit(solution)/shard_map/ppermute | solution.py:23
  30.7 13.2 %copy-start.15 = (f32[4,256,1]{2,1,0:T(8,128)}, f32[4,256,1]{2,1,0:T(8,128)S(1)}, u32[]{:S(2)}) copy-start(f32[4,256,1]{2,1,0:T(8,128)S(1)} %collective-permute-done.6) | copy-start | bytes 12292
  35.0 8.4 %collective-permute-start.8 = (f32[4,1,130]{2,1,0:T(1,128)S(1)}, f32[4,1,130]{2,1,0:T(1,128)S(1)}, u32[]{:S(2)}, u32[]{:S(2)}) collective-permute-start(f32[4,1,130]{2,1,0:T(1,128)S(1)} %get-tuple-element.35), channel_id=1, source_target_pairs={{0,2},{1,3},{4,6},{5,7},{8,10},{9,11},{12,14},{13,15},{16,18},{17,... | collective-permute-start | bytes 6248 | tf_op jit(solution)/shard_map/ppermute | solution.py:22
  38.4 5.5 %collective-permute-start.9 = (f32[4,1,130]{2,1,0:T(1,128)S(1)}, f32[4,1,130]{2,1,0:T(1,128)S(1)}, u32[]{:S(2)}, u32[]{:S(2)}) collective-permute-start(f32[4,1,130]{2,1,0:T(1,128)S(1)} %get-tuple-element.36), channel_id=1, source_target_pairs={{2,0},{3,1},{6,4},{7,5},{10,8},{11,9},{14,12},{15,13},{18,16},{19,... | collective-permute-start | bytes 6248 | tf_op jit(solution)/shard_map/ppermute | solution.py:23
  40.9 8.7 %collective-permute-start.4 = (f32[1,258,130]{2,1,0:T(8,128)}, f32[1,258,130]{2,1,0:T(8,128)S(1)}, u32[]{:S(2)}, u32[]{:S(2)}) collective-permute-start(f32[1,258,130]{2,1,0:T(8,128)} %get-tuple-element.26), channel_id=1, source_target_pairs={{0,1},{2,3},{4,5},{6,7},{8,9},{10,11},{12,13},{14,15},{16,17},{18,... | collective-permute-start | bytes 402488 | tf_op jit(solution)/shard_map/ppermute | solution.py:22
  42.2 7.4 %collective-permute-start.5 = (f32[1,258,130]{2,1,0:T(8,128)}, f32[1,258,130]{2,1,0:T(8,128)S(1)}, u32[]{:S(2)}, u32[]{:S(2)}) collective-permute-start(f32[1,258,130]{2,1,0:T(8,128)} %get-tuple-element.25), channel_id=1, source_target_pairs={{1,0},{3,2},{5,4},{7,6},{9,8},{11,10},{13,12},{15,14},{17,16},{19,... | collective-permute-start | bytes 402488 | tf_op jit(solution)/shard_map/ppermute | solution.py:23
  44.2 5.3 %collective-permute-start.10 = (f32[1,258,130]{2,1,0:T(8,128)S(1)}, f32[1,258,130]{2,1,0:T(8,128)S(1)}, u32[]{:S(2)}, u32[]{:S(2)}) collective-permute-start(f32[1,258,130]{2,1,0:T(8,128)S(1)} %get-tuple-element.27), channel_id=1, source_target_pairs={{0,1},{2,3},{4,5},{6,7},{8,9},{10,11},{12,13},{14,15},{16,17},{18,... | collective-permute-start | bytes 402488 | tf_op jit(solution)/shard_map/ppermute | solution.py:22
  46.9 4.1 %collective-permute-start.11 = (f32[1,258,130]{2,1,0:T(8,128)S(1)}, f32[1,258,130]{2,1,0:T(8,128)}, u32[]{:S(2)}, u32[]{:S(2)}) collective-permute-start(f32[1,258,130]{2,1,0:T(8,128)S(1)} %get-tuple-element.28), channel_id=1, source_target_pairs={{1,0},{3,2},{5,4},{7,6},{9,8},{11,10},{13,12},{15,14},{17,16},{19,... | collective-permute-start | bytes 402488 | tf_op jit(solution)/shard_map/ppermute | solution.py:23
  58.0 36.8 %copy-start = (f32[4,256,128]{2,1,0:T(8,128)}, f32[4,256,128]{2,1,0:T(8,128)S(1)}, u32[]{:S(2)}) copy-start(f32[4,256,128]{2,1,0:T(8,128)S(1)} %get-tuple-element.13) | copy-start | bytes 1572868
  58.1 36.8 %copy-start.9 = (f32[4,256,128]{2,1,0:T(8,128)}, f32[4,256,128]{2,1,0:T(8,128)S(1)}, u32[]{:S(2)}) copy-start(f32[4,256,128]{2,1,0:T(8,128)S(1)} %get-tuple-element.15) | copy-start | bytes 1572868
  58.1 36.8 %copy-start.11 = (f32[4,256,128]{2,1,0:T(8,128)}, f32[4,256,128]{2,1,0:T(8,128)S(1)}, u32[]{:S(2)}) copy-start(f32[4,256,128]{2,1,0:T(8,128)S(1)} %get-tuple-element.16) | copy-start | bytes 1572868
  60.0 14.9 %collective-permute-start.12 = (f32[4,256,1]{2,1,0:T(8,128)S(1)}, f32[4,256,1]{2,1,0:T(8,128)S(1)}, u32[]{:S(2)}, u32[]{:S(2)}) collective-permute-start(f32[4,256,1]{2,1,0:T(8,128)S(1)} %get-tuple-element.39), channel_id=1, source_target_pairs={{0,4},{4,8},{8,12},{1,5},{5,9},{9,13},{2,6},{6,10},{10,14},{3,7},{... | collective-permute-start | bytes 12296 | tf_op jit(solution)/shard_map/ppermute | solution.py:22
  63.5 16.1 %collective-permute-start.13 = (f32[4,256,1]{2,1,0:T(8,128)S(1)}, f32[4,256,1]{2,1,0:T(8,128)S(1)}, u32[]{:S(2)}, u32[]{:S(2)}) collective-permute-start(f32[4,256,1]{2,1,0:T(8,128)S(1)} %get-tuple-element.40), channel_id=1, source_target_pairs={{4,0},{8,4},{12,8},{5,1},{9,5},{13,9},{6,2},{10,6},{14,10},{7,3},{... | collective-permute-start | bytes 12296 | tf_op jit(solution)/shard_map/ppermute | solution.py:23
  79.7 5.9 %collective-permute-start.14 = (f32[4,1,130]{2,1,0:T(1,128)S(1)}, f32[4,1,130]{2,1,0:T(1,128)S(1)}, u32[]{:S(2)}, u32[]{:S(2)}) collective-permute-start(f32[4,1,130]{2,1,0:T(1,128)S(1)} %get-tuple-element.31), channel_id=1, source_target_pairs={{0,2},{1,3},{4,6},{5,7},{8,10},{9,11},{12,14},{13,15},{16,18},{17,... | collective-permute-start | bytes 6248 | tf_op jit(solution)/shard_map/ppermute | solution.py:22
  84.3 5.5 %collective-permute-start.15 = (f32[4,1,130]{2,1,0:T(1,128)S(1)}, f32[4,1,130]{2,1,0:T(1,128)S(1)}, u32[]{:S(2)}, u32[]{:S(2)}) collective-permute-start(f32[4,1,130]{2,1,0:T(1,128)S(1)} %get-tuple-element.32), channel_id=1, source_target_pairs={{2,0},{3,1},{6,4},{7,5},{10,8},{11,9},{14,12},{15,13},{18,16},{19,... | collective-permute-start | bytes 6248 | tf_op jit(solution)/shard_map/ppermute | solution.py:23
  90.1 2.6 %collective-permute-start.16 = (f32[1,258,130]{2,1,0:T(8,128)S(1)}, f32[1,258,130]{2,1,0:T(8,128)S(1)}, u32[]{:S(2)}, u32[]{:S(2)}) collective-permute-start(f32[1,258,130]{2,1,0:T(8,128)S(1)} %get-tuple-element.23), channel_id=1, source_target_pairs={{0,1},{2,3},{4,5},{6,7},{8,9},{10,11},{12,13},{14,15},{16,17},{18,... | collective-permute-start | bytes 402488 | tf_op jit(solution)/shard_map/ppermute | solution.py:22
  91.4 3.4 %collective-permute-start.17 = (f32[1,258,130]{2,1,0:T(8,128)S(1)}, f32[1,258,130]{2,1,0:T(8,128)S(1)}, u32[]{:S(2)}, u32[]{:S(2)}) collective-permute-start(f32[1,258,130]{2,1,0:T(8,128)S(1)} %get-tuple-element.24), channel_id=1, source_target_pairs={{1,0},{3,2},{5,4},{7,6},{9,8},{11,10},{13,12},{15,14},{17,16},{19,... | collective-permute-start | bytes 402488 | tf_op jit(solution)/shard_map/ppermute | solution.py:23
  133.2 29.1 %copy-start.6 = (f32[4,256,128]{2,1,0:T(8,128)}, f32[4,256,128]{2,1,0:T(8,128)S(1)}, u32[]{:S(2)}) copy-start(f32[4,256,128]{2,1,0:T(8,128)S(1)} %multiply_subtract_fusion.1) | copy-start | bytes 1572868
  133.4 12.6 %collective-permute-start.18 = (f32[4,256,1]{2,1,0:T(8,128)S(1)}, f32[4,256,1]{2,1,0:T(8,128)S(1)}, u32[]{:S(2)}, u32[]{:S(2)}) collective-permute-start(f32[4,256,1]{2,1,0:T(8,128)S(1)} %get-tuple-element.37), channel_id=1, source_target_pairs={{0,4},{4,8},{8,12},{1,5},{5,9},{9,13},{2,6},{6,10},{10,14},{3,7},{... | collective-permute-start | bytes 12296 | tf_op jit(solution)/shard_map/ppermute | solution.py:22
  134.7 15.5 %collective-permute-start.19 = (f32[4,256,1]{2,1,0:T(8,128)S(1)}, f32[4,256,1]{2,1,0:T(8,128)S(1)}, u32[]{:S(2)}, u32[]{:S(2)}) collective-permute-start(f32[4,256,1]{2,1,0:T(8,128)S(1)} %get-tuple-element.38), channel_id=1, source_target_pairs={{4,0},{8,4},{12,8},{5,1},{9,5},{13,9},{6,2},{10,6},{14,10},{7,3},{... | collective-permute-start | bytes 12296 | tf_op jit(solution)/shard_map/ppermute | solution.py:23
  150.3 2.8 %collective-permute-start.20 = (f32[4,1,130]{2,1,0:T(1,128)S(1)}, f32[4,1,130]{2,1,0:T(1,128)S(1)}, u32[]{:S(2)}, u32[]{:S(2)}) collective-permute-start(f32[4,1,130]{2,1,0:T(1,128)S(1)} %get-tuple-element.29), channel_id=1, source_target_pairs={{0,2},{1,3},{4,6},{5,7},{8,10},{9,11},{12,14},{13,15},{16,18},{17,... | collective-permute-start | bytes 6248 | tf_op jit(solution)/shard_map/ppermute | solution.py:22
  151.6 5.6 %collective-permute-start.21 = (f32[4,1,130]{2,1,0:T(1,128)S(1)}, f32[4,1,130]{2,1,0:T(1,128)S(1)}, u32[]{:S(2)}, u32[]{:S(2)}) collective-permute-start(f32[4,1,130]{2,1,0:T(1,128)S(1)} %get-tuple-element.30), channel_id=1, source_target_pairs={{2,0},{3,1},{6,4},{7,5},{10,8},{11,9},{14,12},{15,13},{18,16},{19,... | collective-permute-start | bytes 6248 | tf_op jit(solution)/shard_map/ppermute | solution.py:23
  157.5 2.6 %collective-permute-start.22 = (f32[1,258,130]{2,1,0:T(8,128)S(1)}, f32[1,258,130]{2,1,0:T(8,128)S(1)}, u32[]{:S(2)}, u32[]{:S(2)}) collective-permute-start(f32[1,258,130]{2,1,0:T(8,128)S(1)} %get-tuple-element.21), channel_id=1, source_target_pairs={{0,1},{2,3},{4,5},{6,7},{8,9},{10,11},{12,13},{14,15},{16,17},{18,... | collective-permute-start | bytes 402488 | tf_op jit(solution)/shard_map/ppermute | solution.py:22
  158.8 3.4 %collective-permute-start.23 = (f32[1,258,130]{2,1,0:T(8,128)S(1)}, f32[1,258,130]{2,1,0:T(8,128)S(1)}, u32[]{:S(2)}, u32[]{:S(2)}) collective-permute-start(f32[1,258,130]{2,1,0:T(8,128)S(1)} %get-tuple-element.22), channel_id=1, source_target_pairs={{1,0},{3,2},{5,4},{7,6},{9,8},{11,10},{13,12},{15,14},{17,16},{19,... | collective-permute-start | bytes 402488 | tf_op jit(solution)/shard_map/ppermute | solution.py:23
  (17 other events, 113.5 us)
where the time goes:
time: 203 us
  blocking collectives  60.5 us (30%)
  waiting for transfers between devices  54.7 us (27%)
  starting transfers between devices  49.4 us (24%)
  other arithmetic  23.4 us (12%)
  local copies, waits for them, and re-layouts  7.08 us (3%)
  between operations  6.83 us (3%)
    psum x2, blocking collectives, body(): lax.psum((jnp.sum(leftover_misfit * smoothed), jnp.sum(applied * smoothed...  60.5 us
    ppermute x12, starting transfers between devices, with_halo(): before = lax.ppermute(last, axis, up)  33.6 us
    ppermute x12, waiting for transfers between devices, with_halo(): after = lax.ppermute(first, axis, down)  30.7 us
    ppermute x12, waiting for transfers between devices, with_halo(): before = lax.ppermute(last, axis, up)  24.1 us
    ppermute x12, starting transfers between devices, with_halo(): after = lax.ppermute(first, axis, down)  15.8 us
    div x2, other arithmetic, smooth(): state = damping * vector / diagonal  7.15 us
    reduce_sum x2, other arithmetic, body(): jnp.sum(applied * smoothed)  4.26 us
  transfers between devices with their start and end apart: 24, of which 13 were waited for; matrix products, arithmetic and copies ran while one was open for 2% of the time, Pallas kernels for 0%

commit v1 on v0

--- a/solution.py
+++ b/solution.py
@@ -10,6 +10,11 @@
 coolant_film = 1.5
 band_sink = 1.0
 damping = 0.8
+
+
+def one_after_other(array, inner_axis, outer_axis):
+    half = lax.psum(array, inner_axis)
+    return lax.psum(half, outer_axis)
 
 
 def with_halo(shard, sides, width):
@@ -105,8 +110,8 @@
     smoothed = smooth(leftover_misfit)
     applied = linear_map_action(smoothed)
     for turn in range(ITERS):
-        gamma_now, delta_now = lax.psum(
-            (jnp.sum(leftover_misfit * smoothed), jnp.sum(applied * smoothed)), ("gx", "gy", "gz")
+        gamma_now, delta_now = one_after_other(
+            (jnp.sum(leftover_misfit * smoothed), jnp.sum(applied * smoothed)), ("gy", "gz"), "gx"
         )
         pre = smooth(applied)
         twice = linear_map_action(pre)

time: 203 us -> 175 us (0.86)
  blocking collectives: 60.5 us -> 32.8 us
  waiting for transfers between devices: 54.7 us -> 52.5 us
    psum x2 -> x4, blocking collectives: 60.5 us -> 32.8 us  [the longest x2 19.8 us: one_after_other(): return lax.psum(half, outer_axis)]
    ppermute x12, waiting for transfers between devices: 24.1 us -> 21.7 us  [with_halo(): before = lax.ppermute(last, axis, up)]
    ppermute x12, starting transfers between devices: 33.6 us -> 35.7 us  [with_halo(): before = lax.ppermute(last, axis, up)]
  transfers between devices with their start and end apart: 24 -> 24, of which waited for: 13 -> 13; matrix products, arithmetic and copies ran while one was open for 2% -> 3% of each run, Pallas kernels for 0% -> 0%
where the time goes in v1:
time: 175 us; the launch traced here: 174 us
  waiting for transfers between devices  52.5 us (30%)
  starting transfers between devices  51.4 us (29%)
  blocking collectives  32.8 us (19%)
  other arithmetic  23.3 us (13%)
  local copies, waits for them, and re-layouts  7.1 us (4%)
  between operations  6.95 us (4%)
    ppermute x12, starting transfers between devices, with_halo(): before = lax.ppermute(last, axis, up)  35.7 us
    ppermute x12, waiting for transfers between devices, with_halo(): after = lax.ppermute(first, axis, down)  30.7 us
    ppermute x12, waiting for transfers between devices, with_halo(): before = lax.ppermute(last, axis, up)  21.7 us
    psum x2, blocking collectives, one_after_other(): return lax.psum(half, outer_axis)  19.8 us
    ppermute x12, starting transfers between devices, with_halo(): after = lax.ppermute(first, axis, down)  15.8 us
    psum x2, blocking collectives, one_after_other(): half = lax.psum(array, inner_axis)  12.9 us
    div x2, other arithmetic, smooth(): state = damping * vector / diagonal  6.98 us
    reduce_sum x2, other arithmetic, body(): jnp.sum(applied * smoothed)  4.24 us
  transfers between devices with their start and end apart: 24, of which 13 were waited for; matrix products, arithmetic and copies ran while one was open for 3% of the time, Pallas kernels for 0%

profile of v1, /device:TPU:0, one launch (start us, length us, event | category | flops | bytes accessed | tf_op | source)
XLA Modules:
  0.0 174.5 jit_solution(14735016677569949385)
XLA Ops:
  0.6 2.4 %fusion.120 = (f32[4,256,1]{2,1,0:T(8,128)}, f32[4,256,1]{2,1,0:T(8,128)}) fusion(f32[4,256,128]{2,1,0:T(8,128)} %param.10), kind=kLoop, calls=%fused_computation.277 | loop fusion | bytes 16384 | tf_op jit(solution)/shard_map/slice | solution.py:25
  3.0 5.0 %collective-permute-start = (f32[4,256,1]{2,1,0:T(8,128)}, f32[4,256,1]{2,1,0:T(8,128)S(1)}, u32[]{:S(2)}, u32[]{:S(2)}) collective-permute-start(f32[4,256,1]{2,1,0:T(8,128)} %get-tuple-element.45), channel_id=1, source_target_pairs={{0,4},{4,8},{8,12},{1,5},{5,9},{9,13},{2,6},{6,10},{10,14},{3,7},{... | collective-permute-start | bytes 12296 | tf_op jit(solution)/shard_map/ppermute | solution.py:27
  8.1 1.4 collective-permute-start.1
  10.6 4.7 %collective-permute-start.6 = (f32[4,256,1]{2,1,0:T(8,128)}, f32[4,256,1]{2,1,0:T(8,128)S(1)}, u32[]{:S(2)}, u32[]{:S(2)}) collective-permute-start(f32[4,256,1]{2,1,0:T(8,128)} %get-tuple-element.47), channel_id=1, source_target_pairs={{0,4},{4,8},{8,12},{1,5},{5,9},{9,13},{2,6},{6,10},{10,14},{3,7},{... | collective-permute-start | bytes 12296 | tf_op jit(solution)/shard_map/ppermute | solution.py:27
  17.5 3.1 %collective-permute-done = f32[4,256,1]{2,1,0:T(8,128)S(1)} collective-permute-done((f32[4,256,1]{2,1,0:T(8,128)}, f32[4,256,1]{2,1,0:T(8,128)S(1)}, u32[]{:S(2)}, u32[]{:S(2)}) %collective-permute-start) | collective-permute-done | bytes 4128 | tf_op jit(solution)/shard_map/ppermute | solution.py:27
  20.6 4.5 %collective-permute-done.1 = f32[4,256,1]{2,1,0:T(8,128)S(1)} collective-permute-done((f32[4,256,1]{2,1,0:T(8,128)}, f32[4,256,1]{2,1,0:T(8,128)S(1)}, u32[]{:S(2)}, u32[]{:S(2)}) %collective-permute-start.1) | collective-permute-done | bytes 4128 | tf_op jit(solution)/shard_map/ppermute | solution.py:28
  25.2 3.4 %collective-permute-start.2 = (f32[4,1,130]{2,1,0:T(1,128)S(1)}, f32[4,1,130]{2,1,0:T(1,128)S(1)}, u32[]{:S(2)}, u32[]{:S(2)}) collective-permute-start(f32[4,1,130]{2,1,0:T(1,128)S(1)} %get-tuple-element.37), channel_id=1, source_target_pairs={{0,2},{1,3},{4,6},{5,7},{8,10},{9,11},{12,14},{13,15},{16,18},{17,... | collective-permute-start | bytes 6248 | tf_op jit(solution)/shard_map/ppermute | solution.py:27
  30.7 4.2 %collective-permute-done.7 = f32[4,256,1]{2,1,0:T(8,128)S(1)} collective-permute-done((f32[4,256,1]{2,1,0:T(8,128)}, f32[4,256,1]{2,1,0:T(8,128)S(1)}, u32[]{:S(2)}, u32[]{:S(2)}) %collective-permute-start.7) | collective-permute-done | bytes 4128 | tf_op jit(solution)/shard_map/ppermute | solution.py:28
  35.0 3.4 %collective-permute-start.8 = (f32[4,1,130]{2,1,0:T(1,128)S(1)}, f32[4,1,130]{2,1,0:T(1,128)S(1)}, u32[]{:S(2)}, u32[]{:S(2)}) collective-permute-start(f32[4,1,130]{2,1,0:T(1,128)S(1)} %get-tuple-element.39), channel_id=1, source_target_pairs={{0,2},{1,3},{4,6},{5,7},{8,10},{9,11},{12,14},{13,15},{16,18},{17,... | collective-permute-start | bytes 6248 | tf_op jit(solution)/shard_map/ppermute | solution.py:27
  44.2 2.6 %collective-permute-start.10 = (f32[1,258,130]{2,1,0:T(8,128)S(1)}, f32[1,258,130]{2,1,0:T(8,128)S(1)}, u32[]{:S(2)}, u32[]{:S(2)}) collective-permute-start(f32[1,258,130]{2,1,0:T(8,128)S(1)} %get-tuple-element.31), channel_id=1, source_target_pairs={{0,1},{2,3},{4,5},{6,7},{8,9},{10,11},{12,13},{14,15},{16,17},{18,... | collective-permute-start | bytes 402488 | tf_op jit(solution)/shard_map/ppermute | solution.py:27
  51.0 6.9 %multiply_divide_fusion.1 = (f32[4,256,128]{2,1,0:T(8,128)S(1)}, f32[4,256,128]{2,1,0:T(8,128)S(1)}, f32[4,256,128]{2,1,0:T(8,128)S(1)}, f32[4,256,128]{2,1,0:T(...) fusion(f32[4,256,1]{2,1,0:T(8,128)} %copy-done.16, ...), kind=kLoop, calls=%fused_computation.215 | loop fusion | flops 10878976 | bytes 7381184 | tf_op jit(solution)/shard_map/div | solution.py:97
  59.9 3.5 %collective-permute-start.12 = (f32[4,256,1]{2,1,0:T(8,128)S(1)}, f32[4,256,1]{2,1,0:T(8,128)S(1)}, u32[]{:S(2)}, u32[]{:S(2)}) collective-permute-start(f32[4,256,1]{2,1,0:T(8,128)S(1)} %get-tuple-element.43), channel_id=1, source_target_pairs={{0,4},{4,8},{8,12},{1,5},{5,9},{9,13},{2,6},{6,10},{10,14},{3,7},{... | collective-permute-start | bytes 12296 | tf_op jit(solution)/shard_map/ppermute | solution.py:27
  64.6 10.1 %collective-permute-done.12 = f32[4,256,1]{2,1,0:T(8,128)S(1)} collective-permute-done((f32[4,256,1]{2,1,0:T(8,128)S(1)}, f32[4,256,1]{2,1,0:T(8,128)S(1)}, u32[]{:S(2)}, u32[]{:S(2)}) %collective-permute-start.12) | collective-permute-done | bytes 4128 | tf_op jit(solution)/shard_map/ppermute | solution.py:27
  74.8 4.7 %collective-permute-done.13 = f32[4,256,1]{2,1,0:T(8,128)S(1)} collective-permute-done((f32[4,256,1]{2,1,0:T(8,128)S(1)}, f32[4,256,1]{2,1,0:T(8,128)S(1)}, u32[]{:S(2)}, u32[]{:S(2)}) %collective-permute-start.13) | collective-permute-done | bytes 4128 | tf_op jit(solution)/shard_map/ppermute | solution.py:28
  79.6 4.5 %collective-permute-start.14 = (f32[4,1,130]{2,1,0:T(1,128)S(1)}, f32[4,1,130]{2,1,0:T(1,128)S(1)}, u32[]{:S(2)}, u32[]{:S(2)}) collective-permute-start(f32[4,1,130]{2,1,0:T(1,128)S(1)} %get-tuple-element.35), channel_id=1, source_target_pairs={{0,2},{1,3},{4,6},{5,7},{8,10},{9,11},{12,14},{13,15},{16,18},{17,... | collective-permute-start | bytes 6248 | tf_op jit(solution)/shard_map/ppermute | solution.py:27
  85.4 4.2 %collective-permute-done.15 = f32[4,1,130]{2,1,0:T(1,128)S(1)} collective-permute-done((f32[4,1,130]{2,1,0:T(1,128)S(1)}, f32[4,1,130]{2,1,0:T(1,128)S(1)}, u32[]{:S(2)}, u32[]{:S(2)}) %collective-permute-start.15) | collective-permute-done | bytes 2112 | tf_op jit(solution)/shard_map/ppermute | solution.py:28
  92.5 2.1 %collective-permute-done.17 = f32[1,258,130]{2,1,0:T(8,128)S(1)} collective-permute-done((f32[1,258,130]{2,1,0:T(8,128)S(1)}, f32[1,258,130]{2,1,0:T(8,128)S(1)}, u32[]{:S(2)}, u32[]{:S(2)}) %collective-permute-start.17) | collective-permute-done | bytes 134192 | tf_op jit(solution)/shard_map/ppermute | solution.py:28
  94.7 1.8 %multiply_reduce_fusion.2 = (f32[]{:T(128)}, f32[]{:T(128)}, f32[4,256,128]{2,1,0:T(8,128)S(1)}) fusion(f32[4,256,128]{2,1,0:T(8,128)S(1)} %fusion.32, f32[4,256,128]{2,1,0:T(8,128)S(1)} %get-tuple-element.17, f32[4,256,128]{2,1,0:T(8,128)S(1)} %get-tuple-element.24, f32[4,256,1]{2,1,0:T(8,128)S(1)} %collective-permute-done.13, ...), kind=kLoop, calls=%fused_computation.213 | loop fusion | flops 4587518 | bytes 5523560 | tf_op jit(solution)/shard_map/reduce_sum | solution.py:114
  98.6 6.5 %all-reduce.7 = (f32[]{:T(128)}, f32[]{:T(128)}) all-reduce(f32[]{:T(128)} %get-tuple-element.5, f32[]{:T(128)} %get-tuple-element.4), channel_id=1, replica_groups=mesh['groups'=2,'gx'=4,'gy'=2,'gz'=2] {'gy','gz'}, use_global_device_ids=true, to_apply=%region_1.2 | all-reduce | flops 2 | bytes 16 | tf_op jit(solution)/shard_map/psum | solution.py:16
  105.1 10.6 %all-reduce.9 = (f32[]{:T(128)}, f32[]{:T(128)}) all-reduce(f32[]{:T(128)} %get-tuple-element.8, f32[]{:T(128)} %get-tuple-element.9), channel_id=1, replica_groups=mesh['groups'=2,'gx'=4,'gy'=2,'gz'=2] {'gx'}, use_global_device_ids=true, to_apply=%region_2.3 | all-reduce | flops 2 | bytes 16 | tf_op jit(solution)/shard_map/psum | solution.py:17
  117.0 2.9 %multiply_subtract_fusion.1 = f32[4,256,128]{2,1,0:T(8,128)S(1)} fusion(f32[4,256,128]{2,1,0:T(8,128)S(1)} %fusion.32, f32[4,256,128]{2,1,0:T(8,128)} %fusion.56, f32[4,256,128]{2,1,0:T(8,128)S(1)} %get-tuple-element.18, f32[4,256,128]{2,1,0:T(8,128)} %copy-done.3, f32[4,256,128]{2,1,0:T(8,128)S(1)} %get-tuple-element.24, ...), kind=kLoop, calls=%fused_computation.210 | loop fusion | flops 2490368 | bytes 4722692 | tf_op jit(solution)/shard_map/sub | solution.py:138
  120.1 2.4 %collective-permute-start.18 = (f32[4,256,1]{2,1,0:T(8,128)S(1)}, f32[4,256,1]{2,1,0:T(8,128)S(1)}, u32[]{:S(2)}, u32[]{:S(2)}) collective-permute-start(f32[4,256,1]{2,1,0:T(8,128)S(1)} %get-tuple-element.41), channel_id=1, source_target_pairs={{0,4},{4,8},{8,12},{1,5},{5,9},{9,13},{2,6},{6,10},{10,14},{3,7},{... | collective-permute-start | bytes 12296 | tf_op jit(solution)/shard_map/ppermute | solution.py:27
  123.8 7.7 %collective-permute-done.18 = f32[4,256,1]{2,1,0:T(8,128)S(1)} collective-permute-done((f32[4,256,1]{2,1,0:T(8,128)S(1)}, f32[4,256,1]{2,1,0:T(8,128)S(1)}, u32[]{:S(2)}, u32[]{:S(2)}) %collective-permute-start.18) | collective-permute-done | bytes 4128 | tf_op jit(solution)/shard_map/ppermute | solution.py:27
  131.5 4.1 %collective-permute-done.19 = f32[4,256,1]{2,1,0:T(8,128)S(1)} collective-permute-done((f32[4,256,1]{2,1,0:T(8,128)S(1)}, f32[4,256,1]{2,1,0:T(8,128)S(1)}, u32[]{:S(2)}, u32[]{:S(2)}) %collective-permute-start.19) | collective-permute-done | bytes 4128 | tf_op jit(solution)/shard_map/ppermute | solution.py:28
  135.8 2.3 %collective-permute-start.20 = (f32[4,1,130]{2,1,0:T(1,128)S(1)}, f32[4,1,130]{2,1,0:T(1,128)S(1)}, u32[]{:S(2)}, u32[]{:S(2)}) collective-permute-start(f32[4,1,130]{2,1,0:T(1,128)S(1)} %get-tuple-element.33), channel_id=1, source_target_pairs={{0,2},{1,3},{4,6},{5,7},{8,10},{9,11},{12,14},{13,15},{16,18},{17,... | collective-permute-start | bytes 6248 | tf_op jit(solution)/shard_map/ppermute | solution.py:27
  138.1 1.4 collective-permute-start.21
  139.6 4.2 %collective-permute-done.21 = f32[4,1,130]{2,1,0:T(1,128)S(1)} collective-permute-done((f32[4,1,130]{2,1,0:T(1,128)S(1)}, f32[4,1,130]{2,1,0:T(1,128)S(1)}, u32[]{:S(2)}, u32[]{:S(2)}) %collective-permute-start.21) | collective-permute-done | bytes 2112 | tf_op jit(solution)/shard_map/ppermute | solution.py:28
  146.7 2.1 %collective-permute-done.23 = f32[1,258,130]{2,1,0:T(8,128)S(1)} collective-permute-done((f32[1,258,130]{2,1,0:T(8,128)S(1)}, f32[1,258,130]{2,1,0:T(8,128)S(1)}, u32[]{:S(2)}, u32[]{:S(2)}) %collective-permute-start.23) | collective-permute-done | bytes 134192 | tf_op jit(solution)/shard_map/ppermute | solution.py:28
  148.8 2.5 %multiply_reduce_fusion = (f32[]{:T(128)}, f32[]{:T(128)}, f32[4,256,128]{2,1,0:T(8,128)}) fusion(f32[4,256,128]{2,1,0:T(8,128)S(1)} %multiply_subtract_fusion.1, f32[4,256,128]{2,1,0:T(8,128)S(1)} %copy-done.1, f32[4,256,128]{2,1,0:T(8,128)S(1)} %copy-done.4, f32[]{:T(128)S(6)} %div.69, f32[4,256,128]{2,1,0:T(8,128)S(1)} %get-tuple-element.24, ...), kind=kLoop, calls=%fused_computation.208 | loop fusion | flops 4849662 | bytes 6047852 | tf_op jit(solution)/shard_map/reduce_sum | solution.py:114
  151.3 6.5 %all-reduce.6 = (f32[]{:T(128)}, f32[]{:T(128)}) all-reduce(f32[]{:T(128)} %get-tuple-element.3, f32[]{:T(128)} %get-tuple-element.2), channel_id=1, replica_groups=mesh['groups'=2,'gx'=4,'gy'=2,'gz'=2] {'gy','gz'}, use_global_device_ids=true, to_apply=%region_7.8 | all-reduce | flops 2 | bytes 16 | tf_op jit(solution)/shard_map/psum | solution.py:16
  157.7 9.2 %all-reduce.8 = (f32[]{:T(128)}, f32[]{:T(128)}) all-reduce(f32[]{:T(128)} %get-tuple-element.6, f32[]{:T(128)} %get-tuple-element.7), channel_id=1, replica_groups=mesh['groups'=2,'gx'=4,'gy'=2,'gz'=2] {'gx'}, use_global_device_ids=true, to_apply=%region_8.9 | all-reduce | flops 2 | bytes 16 | tf_op jit(solution)/shard_map/psum | solution.py:17
  171.4 2.2 %multiply_add_fusion = f32[4,256,128]{2,1,0:T(8,128)} fusion(f32[4,256,128]{2,1,0:T(8,128)} %copy-done.6, f32[4,256,128]{2,1,0:T(8,128)S(1)} %fusion.32, f32[4,256,128]{2,1,0:T(8,128)} %param.8, f32[]{:T(128)S(6)} %div.74, f32[]{:T(128)S(6)} %div.76, f32[]{:T(128)S(6)} %div.69), kind=kLoop, calls=%fused_computation.207 | loop fusion | flops 786432 | bytes 2097164 | tf_op jit(solution)/shard_map/add | solution.py:135
  (112 shorter events, 30.4 us)
Async XLA Ops:
  3.0 17.6 %collective-permute-start = (f32[4,256,1]{2,1,0:T(8,128)}, f32[4,256,1]{2,1,0:T(8,128)S(1)}, u32[]{:S(2)}, u32[]{:S(2)}) collective-permute-start(f32[4,256,1]{2,1,0:T(8,128)} %get-tuple-element.45), channel_id=1, source_target_pairs={{0,4},{4,8},{8,12},{1,5},{5,9},{9,13},{2,6},{6,10},{10,14},{3,7},{... | collective-permute-start | bytes 12296 | tf_op jit(solution)/shard_map/ppermute | solution.py:27
  8.1 17.0 %collective-permute-start.1 = (f32[4,256,1]{2,1,0:T(8,128)}, f32[4,256,1]{2,1,0:T(8,128)S(1)}, u32[]{:S(2)}, u32[]{:S(2)}) collective-permute-start(f32[4,256,1]{2,1,0:T(8,128)} %get-tuple-element.46), channel_id=1, source_target_pairs={{4,0},{8,4},{12,8},{5,1},{9,5},{13,9},{6,2},{10,6},{14,10},{7,3},{... | collective-permute-start | bytes 12296 | tf_op jit(solution)/shard_map/ppermute | solution.py:28
  10.6 14.5 %copy-start.8 = (f32[4,256,128]{2,1,0:T(8,128)S(1)}, f32[4,256,128]{2,1,0:T(8,128)}, u32[]{:S(2)}) copy-start(f32[4,256,128]{2,1,0:T(8,128)} %param.10) | copy-start | bytes 1572868
  10.6 20.1 %collective-permute-start.6 = (f32[4,256,1]{2,1,0:T(8,128)}, f32[4,256,1]{2,1,0:T(8,128)S(1)}, u32[]{:S(2)}, u32[]{:S(2)}) collective-permute-start(f32[4,256,1]{2,1,0:T(8,128)} %get-tuple-element.47), channel_id=1, source_target_pairs={{0,4},{4,8},{8,12},{1,5},{5,9},{9,13},{2,6},{6,10},{10,14},{3,7},{... | collective-permute-start | bytes 12296 | tf_op jit(solution)/shard_map/ppermute | solution.py:27
  15.3 19.6 %collective-permute-start.7 = (f32[4,256,1]{2,1,0:T(8,128)}, f32[4,256,1]{2,1,0:T(8,128)S(1)}, u32[]{:S(2)}, u32[]{:S(2)}) collective-permute-start(f32[4,256,1]{2,1,0:T(8,128)} %get-tuple-element.48), channel_id=1, source_target_pairs={{4,0},{8,4},{12,8},{5,1},{9,5},{13,9},{6,2},{10,6},{14,10},{7,3},{... | collective-permute-start | bytes 12296 | tf_op jit(solution)/shard_map/ppermute | solution.py:28
  20.6 19.2 %copy-start.13 = (f32[4,256,1]{2,1,0:T(8,128)}, f32[4,256,1]{2,1,0:T(8,128)S(1)}, u32[]{:S(2)}) copy-start(f32[4,256,1]{2,1,0:T(8,128)S(1)} %collective-permute-done) | copy-start | bytes 12292
  25.1 14.7 %copy-start.14 = (f32[4,256,1]{2,1,0:T(8,128)}, f32[4,256,1]{2,1,0:T(8,128)S(1)}, u32[]{:S(2)}) copy-start(f32[4,256,1]{2,1,0:T(8,128)S(1)} %collective-permute-done.1) | copy-start | bytes 12292
  25.2 14.5 %collective-permute-start.2 = (f32[4,1,130]{2,1,0:T(1,128)S(1)}, f32[4,1,130]{2,1,0:T(1,128)S(1)}, u32[]{:S(2)}, u32[]{:S(2)}) collective-permute-start(f32[4,1,130]{2,1,0:T(1,128)S(1)} %get-tuple-element.37), channel_id=1, source_target_pairs={{0,2},{1,3},{4,6},{5,7},{8,10},{9,11},{12,14},{13,15},{16,18},{17,... | collective-permute-start | bytes 6248 | tf_op jit(solution)/shard_map/ppermute | solution.py:27
  28.6 11.1 %collective-permute-start.3 = (f32[4,1,130]{2,1,0:T(1,128)S(1)}, f32[4,1,130]{2,1,0:T(1,128)S(1)}, u32[]{:S(2)}, u32[]{:S(2)}) collective-permute-start(f32[4,1,130]{2,1,0:T(1,128)S(1)} %get-tuple-element.38), channel_id=1, source_target_pairs={{2,0},{3,1},{6,4},{7,5},{10,8},{11,9},{14,12},{15,13},{18,16},{19,... | collective-permute-start | bytes 6248 | tf_op jit(solution)/shard_map/ppermute | solution.py:28
  30.7 13.2 %copy-start.15 = (f32[4,256,1]{2,1,0:T(8,128)}, f32[4,256,1]{2,1,0:T(8,128)S(1)}, u32[]{:S(2)}) copy-start(f32[4,256,1]{2,1,0:T(8,128)S(1)} %collective-permute-done.6) | copy-start | bytes 12292
  35.0 8.4 %collective-permute-start.8 = (f32[4,1,130]{2,1,0:T(1,128)S(1)}, f32[4,1,130]{2,1,0:T(1,128)S(1)}, u32[]{:S(2)}, u32[]{:S(2)}) collective-permute-start(f32[4,1,130]{2,1,0:T(1,128)S(1)} %get-tuple-element.39), channel_id=1, source_target_pairs={{0,2},{1,3},{4,6},{5,7},{8,10},{9,11},{12,14},{13,15},{16,18},{17,... | collective-permute-start | bytes 6248 | tf_op jit(solution)/shard_map/ppermute | solution.py:27
  38.4 5.5 %collective-permute-start.9 = (f32[4,1,130]{2,1,0:T(1,128)S(1)}, f32[4,1,130]{2,1,0:T(1,128)S(1)}, u32[]{:S(2)}, u32[]{:S(2)}) collective-permute-start(f32[4,1,130]{2,1,0:T(1,128)S(1)} %get-tuple-element.40), channel_id=1, source_target_pairs={{2,0},{3,1},{6,4},{7,5},{10,8},{11,9},{14,12},{15,13},{18,16},{19,... | collective-permute-start | bytes 6248 | tf_op jit(solution)/shard_map/ppermute | solution.py:28
  40.9 8.7 %collective-permute-start.4 = (f32[1,258,130]{2,1,0:T(8,128)}, f32[1,258,130]{2,1,0:T(8,128)S(1)}, u32[]{:S(2)}, u32[]{:S(2)}) collective-permute-start(f32[1,258,130]{2,1,0:T(8,128)} %get-tuple-element.30), channel_id=1, source_target_pairs={{0,1},{2,3},{4,5},{6,7},{8,9},{10,11},{12,13},{14,15},{16,17},{18,... | collective-permute-start | bytes 402488 | tf_op jit(solution)/shard_map/ppermute | solution.py:27
  42.2 7.4 %collective-permute-start.5 = (f32[1,258,130]{2,1,0:T(8,128)}, f32[1,258,130]{2,1,0:T(8,128)S(1)}, u32[]{:S(2)}, u32[]{:S(2)}) collective-permute-start(f32[1,258,130]{2,1,0:T(8,128)} %get-tuple-element.29), channel_id=1, source_target_pairs={{1,0},{3,2},{5,4},{7,6},{9,8},{11,10},{13,12},{15,14},{17,16},{19,... | collective-permute-start | bytes 402488 | tf_op jit(solution)/shard_map/ppermute | solution.py:28
  44.2 5.3 %collective-permute-start.10 = (f32[1,258,130]{2,1,0:T(8,128)S(1)}, f32[1,258,130]{2,1,0:T(8,128)S(1)}, u32[]{:S(2)}, u32[]{:S(2)}) collective-permute-start(f32[1,258,130]{2,1,0:T(8,128)S(1)} %get-tuple-element.31), channel_id=1, source_target_pairs={{0,1},{2,3},{4,5},{6,7},{8,9},{10,11},{12,13},{14,15},{16,17},{18,... | collective-permute-start | bytes 402488 | tf_op jit(solution)/shard_map/ppermute | solution.py:27
  46.9 4.1 %collective-permute-start.11 = (f32[1,258,130]{2,1,0:T(8,128)S(1)}, f32[1,258,130]{2,1,0:T(8,128)}, u32[]{:S(2)}, u32[]{:S(2)}) collective-permute-start(f32[1,258,130]{2,1,0:T(8,128)S(1)} %get-tuple-element.32), channel_id=1, source_target_pairs={{1,0},{3,2},{5,4},{7,6},{9,8},{11,10},{13,12},{15,14},{17,16},{19,... | collective-permute-start | bytes 402488 | tf_op jit(solution)/shard_map/ppermute | solution.py:28
  57.9 36.8 %copy-start = (f32[4,256,128]{2,1,0:T(8,128)}, f32[4,256,128]{2,1,0:T(8,128)S(1)}, u32[]{:S(2)}) copy-start(f32[4,256,128]{2,1,0:T(8,128)S(1)} %get-tuple-element.17) | copy-start | bytes 1572868
  57.9 36.8 %copy-start.9 = (f32[4,256,128]{2,1,0:T(8,128)}, f32[4,256,128]{2,1,0:T(8,128)S(1)}, u32[]{:S(2)}) copy-start(f32[4,256,128]{2,1,0:T(8,128)S(1)} %get-tuple-element.19) | copy-start | bytes 1572868
  57.9 36.8 %copy-start.11 = (f32[4,256,128]{2,1,0:T(8,128)}, f32[4,256,128]{2,1,0:T(8,128)S(1)}, u32[]{:S(2)}) copy-start(f32[4,256,128]{2,1,0:T(8,128)S(1)} %get-tuple-element.20) | copy-start | bytes 1572868
  59.9 14.9 %collective-permute-start.12 = (f32[4,256,1]{2,1,0:T(8,128)S(1)}, f32[4,256,1]{2,1,0:T(8,128)S(1)}, u32[]{:S(2)}, u32[]{:S(2)}) collective-permute-start(f32[4,256,1]{2,1,0:T(8,128)S(1)} %get-tuple-element.43), channel_id=1, source_target_pairs={{0,4},{4,8},{8,12},{1,5},{5,9},{9,13},{2,6},{6,10},{10,14},{3,7},{... | collective-permute-start | bytes 12296 | tf_op jit(solution)/shard_map/ppermute | solution.py:27
  63.3 16.1 %collective-permute-start.13 = (f32[4,256,1]{2,1,0:T(8,128)S(1)}, f32[4,256,1]{2,1,0:T(8,128)S(1)}, u32[]{:S(2)}, u32[]{:S(2)}) collective-permute-start(f32[4,256,1]{2,1,0:T(8,128)S(1)} %get-tuple-element.44), channel_id=1, source_target_pairs={{4,0},{8,4},{12,8},{5,1},{9,5},{13,9},{6,2},{10,6},{14,10},{7,3},{... | collective-permute-start | bytes 12296 | tf_op jit(solution)/shard_map/ppermute | solution.py:28
  79.6 5.9 %collective-permute-start.14 = (f32[4,1,130]{2,1,0:T(1,128)S(1)}, f32[4,1,130]{2,1,0:T(1,128)S(1)}, u32[]{:S(2)}, u32[]{:S(2)}) collective-permute-start(f32[4,1,130]{2,1,0:T(1,128)S(1)} %get-tuple-element.35), channel_id=1, source_target_pairs={{0,2},{1,3},{4,6},{5,7},{8,10},{9,11},{12,14},{13,15},{16,18},{17,... | collective-permute-start | bytes 6248 | tf_op jit(solution)/shard_map/ppermute | solution.py:27
  84.1 5.5 %collective-permute-start.15 = (f32[4,1,130]{2,1,0:T(1,128)S(1)}, f32[4,1,130]{2,1,0:T(1,128)S(1)}, u32[]{:S(2)}, u32[]{:S(2)}) collective-permute-start(f32[4,1,130]{2,1,0:T(1,128)S(1)} %get-tuple-element.36), channel_id=1, source_target_pairs={{2,0},{3,1},{6,4},{7,5},{10,8},{11,9},{14,12},{15,13},{18,16},{19,... | collective-permute-start | bytes 6248 | tf_op jit(solution)/shard_map/ppermute | solution.py:28
  89.9 2.6 %collective-permute-start.16 = (f32[1,258,130]{2,1,0:T(8,128)S(1)}, f32[1,258,130]{2,1,0:T(8,128)S(1)}, u32[]{:S(2)}, u32[]{:S(2)}) collective-permute-start(f32[1,258,130]{2,1,0:T(8,128)S(1)} %get-tuple-element.27), channel_id=1, source_target_pairs={{0,1},{2,3},{4,5},{6,7},{8,9},{10,11},{12,13},{14,15},{16,17},{18,... | collective-permute-start | bytes 402488 | tf_op jit(solution)/shard_map/ppermute | solution.py:27
  91.2 3.4 %collective-permute-start.17 = (f32[1,258,130]{2,1,0:T(8,128)S(1)}, f32[1,258,130]{2,1,0:T(8,128)S(1)}, u32[]{:S(2)}, u32[]{:S(2)}) collective-permute-start(f32[1,258,130]{2,1,0:T(8,128)S(1)} %get-tuple-element.28), channel_id=1, source_target_pairs={{1,0},{3,2},{5,4},{7,6},{9,8},{11,10},{13,12},{15,14},{17,16},{19,... | collective-permute-start | bytes 402488 | tf_op jit(solution)/shard_map/ppermute | solution.py:28
  119.9 28.9 %copy-start.6 = (f32[4,256,128]{2,1,0:T(8,128)}, f32[4,256,128]{2,1,0:T(8,128)S(1)}, u32[]{:S(2)}) copy-start(f32[4,256,128]{2,1,0:T(8,128)S(1)} %multiply_subtract_fusion.1) | copy-start | bytes 1572868
  120.1 11.4 %collective-permute-start.18 = (f32[4,256,1]{2,1,0:T(8,128)S(1)}, f32[4,256,1]{2,1,0:T(8,128)S(1)}, u32[]{:S(2)}, u32[]{:S(2)}) collective-permute-start(f32[4,256,1]{2,1,0:T(8,128)S(1)} %get-tuple-element.41), channel_id=1, source_target_pairs={{0,4},{4,8},{8,12},{1,5},{5,9},{9,13},{2,6},{6,10},{10,14},{3,7},{... | collective-permute-start | bytes 12296 | tf_op jit(solution)/shard_map/ppermute | solution.py:27
  122.5 13.2 %collective-permute-start.19 = (f32[4,256,1]{2,1,0:T(8,128)S(1)}, f32[4,256,1]{2,1,0:T(8,128)S(1)}, u32[]{:S(2)}, u32[]{:S(2)}) collective-permute-start(f32[4,256,1]{2,1,0:T(8,128)S(1)} %get-tuple-element.42), channel_id=1, source_target_pairs={{4,0},{8,4},{12,8},{5,1},{9,5},{13,9},{6,2},{10,6},{14,10},{7,3},{... | collective-permute-start | bytes 12296 | tf_op jit(solution)/shard_map/ppermute | solution.py:28
  135.8 3.8 %collective-permute-start.20 = (f32[4,1,130]{2,1,0:T(1,128)S(1)}, f32[4,1,130]{2,1,0:T(1,128)S(1)}, u32[]{:S(2)}, u32[]{:S(2)}) collective-permute-start(f32[4,1,130]{2,1,0:T(1,128)S(1)} %get-tuple-element.33), channel_id=1, source_target_pairs={{0,2},{1,3},{4,6},{5,7},{8,10},{9,11},{12,14},{13,15},{16,18},{17,... | collective-permute-start | bytes 6248 | tf_op jit(solution)/shard_map/ppermute | solution.py:27
  138.1 5.6 %collective-permute-start.21 = (f32[4,1,130]{2,1,0:T(1,128)S(1)}, f32[4,1,130]{2,1,0:T(1,128)S(1)}, u32[]{:S(2)}, u32[]{:S(2)}) collective-permute-start(f32[4,1,130]{2,1,0:T(1,128)S(1)} %get-tuple-element.34), channel_id=1, source_target_pairs={{2,0},{3,1},{6,4},{7,5},{10,8},{11,9},{14,12},{15,13},{18,16},{19,... | collective-permute-start | bytes 6248 | tf_op jit(solution)/shard_map/ppermute | solution.py:28
  144.0 2.6 %collective-permute-start.22 = (f32[1,258,130]{2,1,0:T(8,128)S(1)}, f32[1,258,130]{2,1,0:T(8,128)S(1)}, u32[]{:S(2)}, u32[]{:S(2)}) collective-permute-start(f32[1,258,130]{2,1,0:T(8,128)S(1)} %get-tuple-element.25), channel_id=1, source_target_pairs={{0,1},{2,3},{4,5},{6,7},{8,9},{10,11},{12,13},{14,15},{16,17},{18,... | collective-permute-start | bytes 402488 | tf_op jit(solution)/shard_map/ppermute | solution.py:27
  145.3 3.4 %collective-permute-start.23 = (f32[1,258,130]{2,1,0:T(8,128)S(1)}, f32[1,258,130]{2,1,0:T(8,128)S(1)}, u32[]{:S(2)}, u32[]{:S(2)}) collective-permute-start(f32[1,258,130]{2,1,0:T(8,128)S(1)} %get-tuple-element.26), channel_id=1, source_target_pairs={{1,0},{3,2},{5,4},{7,6},{9,8},{11,10},{13,12},{15,14},{17,16},{19,... | collective-permute-start | bytes 402488 | tf_op jit(solution)/shard_map/ppermute | solution.py:28
  (17 other events, 113.5 us)
